TPU v7x, 32 devices: a whole 2x2x4 slice. The times are simulated.
32 devices in a mesh: ex: 2 (over x), ey: 2 (over y), lin: 8 (over z, core).
Axes of the slice: x: 2, y: 2, z: 4, core: 2. Of those that a mesh axis runs over, the one named last changes fastest.
Arguments:
- load: float32 [5, 5, 5, 4, 16, 256], P(None, None, None, None, ('ey', 'lin'), 'ex'), may hold values from -6 to 6
- kappa: float32 [4, 16, 256], P(None, ('ey', 'lin'), 'ex'), may hold values from 0.3 to 3
- wet: int32 [4, 16, 256], P(None, ('ey', 'lin'), 'ex'), may hold values 0 or 1
Outputs:
- solution: float32 [5, 5, 5, 4, 16, 256], P(None, None, None, None, ('ey', 'lin'), 'ex')
- residual: float32 [5, 5, 5, 4, 16, 256], P(None, None, None, None, ('ey', 'lin'), 'ex')
All inputs are finite; a program needn't handle non-finite values. No bound on the sum of `wet` on one device may be relied on, other than what follows from the above.
Results may differ from a plain program's by a relative error of at most 0.00016.
Values sent between devices are 32-bit elements; how exact they have to be, the bound alone decides.
A program may use at most 64 MiB of HBM per device.

v0:
```python
import math

import jax
import jax.numpy as jnp
import numpy as np
from jax import lax
from jax.sharding import PartitionSpec as P

LOBATTO_NODES = 5
CYCLES = 2
NPRE = 2
NPOST = 2
NC = 4


fine_relax = 0.25
coarse_relax = 0.4


def padded_2(cells, sides, width):
    for axis, dim in sides:
        count = lax.axis_size(axis)
        ends = count - 1
        head = lax.slice_in_dim(cells, 0, width, axis=dim)
        tail = lax.slice_in_dim(cells, cells.shape[dim] - width, cells.shape[dim], axis=dim)
        cells = jnp.concatenate(
            [
                lax.ppermute(tail, axis, [(i, (i + 1) % count) for i in range(ends)]),
                cells,
                lax.ppermute(head, axis, [((i + 1) % count, i) for i in range(ends)]),
            ],
            axis=dim,
        )
    return cells


def node_tables():
    points = np.array([-1.0, -math.sqrt(3.0 / 7.0), 0.0, math.sqrt(3.0 / 7.0), 1.0])
    weights = np.array([0.1, 49.0 / 90.0, 32.0 / 45.0, 49.0 / 90.0, 0.1])
    eye_table = np.eye(points.shape[0])
    spread = points[:, None] - points[None, :] + eye_table
    factors = np.prod(spread, axis=1)
    deriv = factors[:, None] / (factors[None, :] * spread)
    deriv = np.where(eye_table > 0, (np.sum(1.0 / spread, axis=1) - 1.0)[:, None], deriv)
    stiff = deriv.T @ (weights[:, None] * deriv)
    mass = eye_table * weights[:, None]
    interp = np.stack([(1.0 - points) / 2.0, (1.0 + points) / 2.0], axis=1)
    coarse_stiff = interp.T @ stiff @ interp
    coarse_mass = interp.T @ mass @ interp
    return [
        jnp.asarray(table, jnp.float32)
        for table in (stiff, mass, interp, coarse_stiff, coarse_mass)
    ]


def along(matrix, field, axis):
    if axis == 0:
        return jnp.einsum("pa,a...->p...", matrix, field, precision=lax.Precision.HIGHEST)
    if axis == 1:
        return jnp.einsum("qb,ab...->aq...", matrix, field, precision=lax.Precision.HIGHEST)
    return jnp.einsum("rc,abc...->abr...", matrix, field, precision=lax.Precision.HIGHEST)


def element_apply(field, coeff, stiff, mass):
    mass_c = along(mass, field, 2)
    mass_bc = along(mass, mass_c, 1)
    first_term = along(stiff, mass_bc, 0)
    second_term = along(mass, along(stiff, mass_c, 1), 0)
    third_term = along(mass, along(mass, along(stiff, field, 2), 1), 0)
    return coeff * (first_term + second_term + third_term)


def element_diagonal(coeff, stiff, mass):
    stiff_diag = jnp.diagonal(stiff)
    mass_diag = jnp.diagonal(mass)
    local = (
        stiff_diag[:, None, None] * mass_diag[None, :, None] * mass_diag[None, None, :]
        + mass_diag[:, None, None] * stiff_diag[None, :, None] * mass_diag[None, None, :]
        + mass_diag[:, None, None] * mass_diag[None, :, None] * stiff_diag[None, None, :]
    )
    return local[:, :, :, None, None, None] * coeff[None, None, None]


def pair_sum(field, node_axis, fetch):
    count = field.shape[node_axis]
    lower = lax.index_in_dim(field, 0, node_axis, keepdims=False)
    upper = lax.index_in_dim(field, count - 1, node_axis, keepdims=False)
    elem_axis = node_axis + 2
    length = lower.shape[elem_axis]
    lower_first = lax.slice_in_dim(lower, 0, 1, axis=elem_axis)
    upper_last = lax.slice_in_dim(upper, length - 1, length, axis=elem_axis)
    outer = fetch(jnp.concatenate([lower_first, upper_last], axis=elem_axis))
    inner = lax.slice_in_dim(upper, 0, length - 1, axis=elem_axis) + lax.slice_in_dim(
        lower, 1, length, axis=elem_axis
    )
    head = lower_first + lax.slice_in_dim(outer, 0, 1, axis=elem_axis)
    tail = upper_last + lax.slice_in_dim(outer, 3, 4, axis=elem_axis)
    new_lower = jnp.concatenate([head, inner], axis=elem_axis)
    new_upper = jnp.concatenate([inner, tail], axis=elem_axis)
    middle = lax.slice_in_dim(field, 1, count - 1, axis=node_axis)
    return jnp.concatenate(
        [jnp.expand_dims(new_lower, node_axis), middle, jnp.expand_dims(new_upper, node_axis)],
        axis=node_axis,
    )


def pad_edge(axis):

    def padded(edge):
        widths = [(1, 1) if dim == axis else (0, 0) for dim in range(edge.ndim)]
        return jnp.pad(edge, widths)

    return padded


def along_shore(edge):
    return padded_2(edge, (("ex", 4),), 1)


def across_shore(edge):
    return padded_2(edge, ((("ey", "lin"), 3),), 1)


def assemble(field, fetch_x, fetch_y, fetch_z):
    field = pair_sum(field, 2, fetch_x)
    field = pair_sum(field, 1, fetch_y)
    return pair_sum(field, 0, fetch_z)


def surface_mask(count, layers, total):
    node = jnp.arange(count, dtype=jnp.int32)[:, None]
    layer = jnp.arange(layers, dtype=jnp.int32)[None, :]
    keep = jnp.where((node == count - 1) & (layer == total - 1), jnp.float32(0.0), jnp.float32(1.0))
    return keep.reshape(count, 1, 1, layers, 1, 1)


def coarse_sweeps(local, coeff, coarse_sum, keep, inverse, coarse_stiff, coarse_mass):
    restricted = keep * coarse_sum(local)
    correction = inverse * restricted
    for sweep in range(NC - 1):
        image = keep * coarse_sum(element_apply(correction, coeff, coarse_stiff, coarse_mass))
        correction = correction + inverse * (restricted - image)
    return correction


def multigrid(load, coeff, fine_sum, keep, coarse_correct, tables):
    stiff, mass, interp, coarse_stiff, coarse_mass = tables
    inverse = fine_relax / fine_sum(element_diagonal(coeff, stiff, mass))
    rhs = keep * fine_sum(load)
    solution = jnp.zeros_like(load)

    def sweep_once(solution):
        change = keep * fine_sum(load - element_apply(solution, coeff, stiff, mass))
        return solution + inverse * change

    transpose = interp.T
    for cycle in range(CYCLES):
        for sweep in range(NPRE):
            if cycle == 0 and sweep == 0:
                solution = solution + inverse * rhs
            else:
                solution = sweep_once(solution)
        local = load - element_apply(solution, coeff, stiff, mass)
        local = along(transpose, along(transpose, along(transpose, local, 2), 1), 0)
        correction = coarse_correct(local)
        solution = solution + along(interp, along(interp, along(interp, correction, 2), 1), 0)
        for sweep in range(NPOST):
            solution = sweep_once(solution)
    residual = keep * fine_sum(load - element_apply(solution, coeff, stiff, mass))
    return (solution, residual)


def per_device(load, kappa, wet):
    tables = node_tables()
    stiff, mass, interp, coarse_stiff, coarse_mass = tables
    coeff = kappa * jnp.where(wet == 1, jnp.float32(1.0), jnp.float32(0.05))
    layers = coeff.shape[0]

    def block_sum(field):
        return assemble(field, along_shore, across_shore, pad_edge(2))

    fine_retain_mask = surface_mask(LOBATTO_NODES, layers, layers)
    coarse_retain_mask = surface_mask(2, layers, layers)
    coarse_inverse = coarse_relax / block_sum(element_diagonal(coeff, coarse_stiff, coarse_mass))

    def coarse_correct(local):
        return coarse_sweeps(
            local, coeff, block_sum, coarse_retain_mask, coarse_inverse, coarse_stiff, coarse_mass
        )

    return multigrid(load, coeff, block_sum, fine_retain_mask, coarse_correct, tables)


def solution(mesh):
    in_specs = (
        P(None, None, None, None, ("ey", "lin"), "ex"),
        P(None, ("ey", "lin"), "ex"),
        P(None, ("ey", "lin"), "ex"),
    )
    out_specs = (
        P(None, None, None, None, ("ey", "lin"), "ex"),
        P(None, None, None, None, ("ey", "lin"), "ex"),
    )
    return jax.shard_map(
        per_device, mesh=mesh, in_specs=in_specs, out_specs=out_specs, check_vma=False
    )
```

profile of v0, /device:TPU:25, one launch (start us, length us, event | category | flops | bytes accessed | tf_op | source)
XLA Modules:
  0.0 447.1 jit_solution(8701924818879740119)
XLA Ops:
  3.0 3.1 collective-permute-start.12
  12.6 3.1 collective-permute-done.13
  21.0 5.9 %collective-permute-start.2 = (f32[5,5,4,1,128]{4,2,1,0,3:T(4,128)S(1)}, f32[5,5,4,1,128]{4,2,1,0,3:T(4,128)S(1)}, u32[]{:S(2)}, u32[]{:S(2)}) collective-permute-start(f32[5,5,4,1,128]{4,2,1,0,3:T(4,128)S(1)} %maximum_bitcast_fusion.32), channel_id=1, source_target_pairs={{0,1},{1,2},{2,3},{3,4},{4,5},{5,6},{6,7},{7,8},{8,9},{9,10},{10,1... | collective-permute-start | bytes 153608 | tf_op jit(solution)/shard_map/ppermute | solution.py:28
  34.2 3.1 collective-permute-done.3
  51.2 4.2 collective-permute-done.9
  56.6 3.8 collective-permute-start.10
  62.3 3.3 collective-permute-start.15
  65.7 3.1 collective-permute-done.11
  82.7 4.1 collective-permute-start.18
  89.6 6.2 %collective-permute-done.19 = f32[2,2,4,1,128]{4,0,2,1,3:T(2,128)S(1)} collective-permute-done((f32[2,2,4,1,128]{4,0,2,1,3:T(2,128)S(1)}, f32[2,2,4,1,128]{4,0,2,1,3:T(2,128)S(1)}, u32[]{:S(2)}, u32[]{:S(2)}) %collective-permute-start.19) | collective-permute-done | bytes 8224 | tf_op jit(solution)/shard_map/ppermute | solution.py:30
  102.3 3.0 collective-permute-done.21
  105.5 3.9 collective-permute-start.22
  112.2 6.3 %collective-permute-done.23 = f32[2,2,4,1,128]{4,2,1,0,3:T(4,128)S(1)} collective-permute-done((f32[2,2,4,1,128]{4,2,1,0,3:T(4,128)S(1)}, f32[2,2,4,1,128]{4,2,1,0,3:T(4,128)S(1)}, u32[]{:S(2)}, u32[]{:S(2)}) %collective-permute-start.23) | collective-permute-done | bytes 8224 | tf_op jit(solution)/shard_map/ppermute | solution.py:30
  127.0 3.9 collective-permute-start.26
  133.6 6.3 %collective-permute-done.27 = f32[2,2,4,1,128]{4,2,1,0,3:T(4,128)S(1)} collective-permute-done((f32[2,2,4,1,128]{4,2,1,0,3:T(4,128)S(1)}, f32[2,2,4,1,128]{4,2,1,0,3:T(4,128)S(1)}, u32[]{:S(2)}, u32[]{:S(2)}) %collective-permute-start.27) | collective-permute-done | bytes 8224 | tf_op jit(solution)/shard_map/ppermute | solution.py:30
  148.5 3.9 collective-permute-start.30
  155.3 6.1 %collective-permute-done.31 = f32[2,2,4,1,128]{4,2,1,0,3:T(4,128)S(1)} collective-permute-done((f32[2,2,4,1,128]{4,2,1,0,3:T(4,128)S(1)}, f32[2,2,4,1,128]{4,2,1,0,3:T(4,128)S(1)}, u32[]{:S(2)}, u32[]{:S(2)}) %collective-permute-start.31) | collective-permute-done | bytes 8224 | tf_op jit(solution)/shard_map/ppermute | solution.py:30
  172.0 3.5 collective-permute-done.33
  175.7 3.9 collective-permute-start.34
  183.1 6.5 %collective-permute-done.35 = f32[5,5,4,1,128]{4,2,1,0,3:T(4,128)S(1)} collective-permute-done((f32[5,5,4,1,128]{4,2,1,0,3:T(4,128)S(1)}, f32[5,5,4,1,128]{4,2,1,0,3:T(4,128)S(1)}, u32[]{:S(2)}, u32[]{:S(2)}) %collective-permute-start.35) | collective-permute-done | bytes 51232 | tf_op jit(solution)/shard_map/ppermute | solution.py:30
  199.2 3.5 collective-permute-done.37
  202.9 3.9 collective-permute-start.38
  210.0 6.7 %collective-permute-done.39 = f32[5,5,4,1,128]{4,2,1,0,3:T(4,128)S(1)} collective-permute-done((f32[5,5,4,1,128]{4,2,1,0,3:T(4,128)S(1)}, f32[5,5,4,1,128]{4,2,1,0,3:T(4,128)S(1)}, u32[]{:S(2)}, u32[]{:S(2)}) %collective-permute-start.39) | collective-permute-done | bytes 51232 | tf_op jit(solution)/shard_map/ppermute | solution.py:30
  226.7 3.1 collective-permute-done.41
  230.0 3.9 collective-permute-start.42
  237.1 6.7 %collective-permute-done.43 = f32[5,5,4,1,128]{4,2,1,0,3:T(4,128)S(1)} collective-permute-done((f32[5,5,4,1,128]{4,2,1,0,3:T(4,128)S(1)}, f32[5,5,4,1,128]{4,2,1,0,3:T(4,128)S(1)}, u32[]{:S(2)}, u32[]{:S(2)}) %collective-permute-start.43) | collective-permute-done | bytes 51232 | tf_op jit(solution)/shard_map/ppermute | solution.py:30
  253.5 3.5 collective-permute-done.45
  257.2 3.9 collective-permute-start.46
  264.2 6.7 %collective-permute-done.47 = f32[5,5,4,1,128]{4,2,1,0,3:T(4,128)S(1)} collective-permute-done((f32[5,5,4,1,128]{4,2,1,0,3:T(4,128)S(1)}, f32[5,5,4,1,128]{4,2,1,0,3:T(4,128)S(1)}, u32[]{:S(2)}, u32[]{:S(2)}) %collective-permute-start.47) | collective-permute-done | bytes 51232 | tf_op jit(solution)/shard_map/ppermute | solution.py:30
  284.2 3.9 collective-permute-start.50
  290.8 6.3 %collective-permute-done.51 = f32[2,2,4,1,128]{4,2,1,0,3:T(4,128)S(1)} collective-permute-done((f32[2,2,4,1,128]{4,2,1,0,3:T(4,128)S(1)}, f32[2,2,4,1,128]{4,2,1,0,3:T(4,128)S(1)}, u32[]{:S(2)}, u32[]{:S(2)}) %collective-permute-start.51) | collective-permute-done | bytes 8224 | tf_op jit(solution)/shard_map/ppermute | solution.py:30
  302.4 3.0 collective-permute-done.53
  305.6 3.9 collective-permute-start.54
  312.3 6.3 %collective-permute-done.55 = f32[2,2,4,1,128]{4,2,1,0,3:T(4,128)S(1)} collective-permute-done((f32[2,2,4,1,128]{4,2,1,0,3:T(4,128)S(1)}, f32[2,2,4,1,128]{4,2,1,0,3:T(4,128)S(1)}, u32[]{:S(2)}, u32[]{:S(2)}) %collective-permute-start.55) | collective-permute-done | bytes 8224 | tf_op jit(solution)/shard_map/ppermute | solution.py:30
  323.9 3.0 collective-permute-done.57
  327.1 3.9 collective-permute-start.58
  333.8 6.3 %collective-permute-done.59 = f32[2,2,4,1,128]{4,2,1,0,3:T(4,128)S(1)} collective-permute-done((f32[2,2,4,1,128]{4,2,1,0,3:T(4,128)S(1)}, f32[2,2,4,1,128]{4,2,1,0,3:T(4,128)S(1)}, u32[]{:S(2)}, u32[]{:S(2)}) %collective-permute-start.59) | collective-permute-done | bytes 8224 | tf_op jit(solution)/shard_map/ppermute | solution.py:30
  348.6 3.9 collective-permute-start.62
  355.4 6.1 %collective-permute-done.63 = f32[2,2,4,1,128]{4,2,0,1,3:T(4,128)S(1)} collective-permute-done((f32[2,2,4,1,128]{4,2,0,1,3:T(4,128)S(1)}, f32[2,2,4,1,128]{4,2,0,1,3:T(4,128)S(1)}, u32[]{:S(2)}, u32[]{:S(2)}) %collective-permute-start.63) | collective-permute-done | bytes 8224 | tf_op jit(solution)/shard_map/ppermute | solution.py:30
  372.2 3.4 collective-permute-done.65
  375.8 3.9 collective-permute-start.66
  383.1 6.6 %collective-permute-done.67 = f32[5,5,4,1,128]{4,2,0,1,3:T(4,128)S(1)} collective-permute-done((f32[5,5,4,1,128]{4,2,0,1,3:T(4,128)S(1)}, f32[5,5,4,1,128]{4,2,0,1,3:T(4,128)S(1)}, u32[]{:S(2)}, u32[]{:S(2)}) %collective-permute-start.67) | collective-permute-done | bytes 51232 | tf_op jit(solution)/shard_map/ppermute | solution.py:30
  399.4 3.5 collective-permute-done.69
  403.1 3.9 collective-permute-start.70
  410.1 6.8 %collective-permute-done.71 = f32[5,5,4,1,128]{4,2,1,0,3:T(4,128)S(1)} collective-permute-done((f32[5,5,4,1,128]{4,2,1,0,3:T(4,128)S(1)}, f32[5,5,4,1,128]{4,2,1,0,3:T(4,128)S(1)}, u32[]{:S(2)}, u32[]{:S(2)}) %collective-permute-start.71) | collective-permute-done | bytes 51232 | tf_op jit(solution)/shard_map/ppermute | solution.py:30
  426.6 3.4 collective-permute-done.73
  430.3 3.9 collective-permute-start.74
  438.3 5.8 %collective-permute-done.75 = f32[5,5,4,1,128]{4,2,0,1,3:T(4,128)S(1)} collective-permute-done((f32[5,5,4,1,128]{4,2,0,1,3:T(4,128)S(1)}, f32[5,5,4,1,128]{4,2,0,1,3:T(4,128)S(1)}, u32[]{:S(2)}, u32[]{:S(2)}) %collective-permute-start.75) | collective-permute-done | bytes 51232 | tf_op jit(solution)/shard_map/ppermute | solution.py:30
  (644 shorter events, 224.9 us)
Async XLA Ops:
  3.0 8.3 %collective-permute-start.12 = (f32[2,2,4,1,1]{4,2,0,1,3:T(4,128)S(1)}, f32[2,2,4,1,1]{4,2,0,1,3:T(4,128)S(1)}, u32[]{:S(2)}, u32[]{:S(2)}) collective-permute-start(f32[2,2,4,1,1]{4,2,0,1,3:T(4,128)S(1)} %slice.1268), channel_id=1, source_target_pairs={{0,16},{1,17},{2,18},{3,19},{4,20},{5,21},{6,22},{7,23},{8,24},{9,... | collective-permute-start | bytes 200 | tf_op jit(solution)/shard_map/ppermute | solution.py:28
  8.0 7.9 %collective-permute-start = (f32[5,5,4,1,1]{4,2,0,1,3:T(4,128)S(1)}, f32[5,5,4,1,1]{4,2,0,1,3:T(4,128)S(1)}, u32[]{:S(2)}, u32[]{:S(2)}) collective-permute-start(f32[5,5,4,1,1]{4,2,0,1,3:T(4,128)S(1)} %slice.1233), channel_id=1, source_target_pairs={{0,16},{1,17},{2,18},{3,19},{4,20},{5,21},{6,22},{7,23},{8,24},{9,... | collective-permute-start | bytes 1208 | tf_op jit(solution)/shard_map/ppermute | solution.py:28
  9.4 7.7 %collective-permute-start.4 = (f32[5,5,4,1,1]{4,2,0,1,3:T(4,128)S(1)}, f32[5,5,4,1,1]{4,2,0,1,3:T(4,128)S(1)}, u32[]{:S(2)}, u32[]{:S(2)}) collective-permute-start(f32[5,5,4,1,1]{4,2,0,1,3:T(4,128)S(1)} %slice.1244), channel_id=1, source_target_pairs={{0,16},{1,17},{2,18},{3,19},{4,20},{5,21},{6,22},{7,23},{8,24},{9,... | collective-permute-start | bytes 1208 | tf_op jit(solution)/shard_map/ppermute | solution.py:28
  15.9 4.9 %collective-permute-start.1 = (f32[5,5,4,1,1]{4,2,0,1,3:T(4,128)S(1)}, f32[5,5,4,1,1]{4,2,0,1,3:T(4,128)S(1)}, u32[]{:S(2)}, u32[]{:S(2)}) collective-permute-start(f32[5,5,4,1,1]{4,2,0,1,3:T(4,128)S(1)} %get-tuple-element.143), channel_id=1, source_target_pairs={{16,0},{17,1},{18,2},{19,3},{20,4},{21,5},{22,6},{23,7},{24,8},{25... | collective-permute-start | bytes 1208 | tf_op jit(solution)/shard_map/ppermute | solution.py:30
  17.2 9.8 %collective-permute-start.5 = (f32[5,5,4,1,1]{4,2,0,1,3:T(4,128)S(1)}, f32[5,5,4,1,1]{4,2,0,1,3:T(4,128)S(1)}, u32[]{:S(2)}, u32[]{:S(2)}) collective-permute-start(f32[5,5,4,1,1]{4,2,0,1,3:T(4,128)S(1)} %get-tuple-element.149), channel_id=1, source_target_pairs={{16,0},{17,1},{18,2},{19,3},{20,4},{21,5},{22,6},{23,7},{24,8},{25... | collective-permute-start | bytes 1208 | tf_op jit(solution)/shard_map/ppermute | solution.py:30
  21.0 8.1 %collective-permute-start.2 = (f32[5,5,4,1,128]{4,2,1,0,3:T(4,128)S(1)}, f32[5,5,4,1,128]{4,2,1,0,3:T(4,128)S(1)}, u32[]{:S(2)}, u32[]{:S(2)}) collective-permute-start(f32[5,5,4,1,128]{4,2,1,0,3:T(4,128)S(1)} %maximum_bitcast_fusion.32), channel_id=1, source_target_pairs={{0,1},{1,2},{2,3},{3,4},{4,5},{5,6},{6,7},{7,8},{8,9},{9,10},{10,1... | collective-permute-start | bytes 153608 | tf_op jit(solution)/shard_map/ppermute | solution.py:28
  29.2 8.1 %collective-permute-start.3 = (f32[5,5,4,1,128]{4,2,1,0,3:T(4,128)S(1)}, f32[5,5,4,1,128]{4,2,1,0,3:T(4,128)S(1)}, u32[]{:S(2)}, u32[]{:S(2)}) collective-permute-start(f32[5,5,4,1,128]{4,2,1,0,3:T(4,128)S(1)} %get-tuple-element.43), channel_id=1, source_target_pairs={{1,0},{2,1},{3,2},{4,3},{5,4},{6,5},{7,6},{8,7},{9,8},{10,9},{11,1... | collective-permute-start | bytes 153608 | tf_op jit(solution)/shard_map/ppermute | solution.py:30
  31.7 8.3 %collective-permute-start.7 = (f32[5,5,4,1,128]{4,2,1,0,3:T(4,128)S(1)}, f32[5,5,4,1,128]{4,2,1,0,3:T(4,128)S(1)}, u32[]{:S(2)}, u32[]{:S(2)}) collective-permute-start(f32[5,5,4,1,128]{4,2,1,0,3:T(4,128)S(1)} %get-tuple-element.41), channel_id=1, source_target_pairs={{1,0},{2,1},{3,2},{4,3},{5,4},{6,5},{7,6},{8,7},{9,8},{10,9},{11,1... | collective-permute-start | bytes 153608 | tf_op jit(solution)/shard_map/ppermute | solution.py:30
  47.6 14.8 %collective-permute-start.14 = (f32[2,2,4,1,128]{4,2,1,0,3:T(4,128)S(1)}, f32[2,2,4,1,128]{4,2,1,0,3:T(4,128)S(1)}, u32[]{:S(2)}, u32[]{:S(2)}) collective-permute-start(f32[2,2,4,1,128]{4,2,1,0,3:T(4,128)S(1)} %fusion.302), channel_id=1, source_target_pairs={{0,1},{1,2},{2,3},{3,4},{4,5},{5,6},{6,7},{7,8},{8,9},{9,10},{10,1... | collective-permute-start | bytes 24584 | tf_op jit(solution)/shard_map/ppermute | solution.py:28
  49.8 5.7 %collective-permute-start.9 = (f32[5,5,4,1,1]{4,0,2,1,3:T(8,128)S(1)}, f32[5,5,4,1,1]{4,0,2,1,3:T(8,128)S(1)}, u32[]{:S(2)}, u32[]{:S(2)}) collective-permute-start(f32[5,5,4,1,1]{4,0,2,1,3:T(8,128)S(1)} %get-tuple-element.93), channel_id=1, source_target_pairs={{16,0},{17,1},{18,2},{19,3},{20,4},{21,5},{22,6},{23,7},{24,8},{25... | collective-permute-start | bytes 1208 | tf_op jit(solution)/shard_map/ppermute | solution.py:30
  56.6 9.1 %collective-permute-start.10 = (f32[5,5,4,1,128]{4,0,2,1,3:T(8,128)S(1)}, f32[5,5,4,1,128]{4,0,2,1,3:T(8,128)S(1)}, u32[]{:S(2)}, u32[]{:S(2)}) collective-permute-start(f32[5,5,4,1,128]{4,0,2,1,3:T(8,128)S(1)} %get-tuple-element.48), channel_id=1, source_target_pairs={{0,1},{1,2},{2,3},{3,4},{4,5},{5,6},{6,7},{7,8},{8,9},{9,10},{10,1... | collective-permute-start | bytes 153608 | tf_op jit(solution)/shard_map/ppermute | solution.py:28
  60.4 8.5 %collective-permute-start.11 = (f32[5,5,4,1,128]{4,0,2,1,3:T(8,128)S(1)}, f32[5,5,4,1,128]{4,0,2,1,3:T(8,128)S(1)}, u32[]{:S(2)}, u32[]{:S(2)}) collective-permute-start(f32[5,5,4,1,128]{4,0,2,1,3:T(8,128)S(1)} %get-tuple-element.49), channel_id=1, source_target_pairs={{1,0},{2,1},{3,2},{4,3},{5,4},{6,5},{7,6},{8,7},{9,8},{10,9},{11,1... | collective-permute-start | bytes 153608 | tf_op jit(solution)/shard_map/ppermute | solution.py:30
  62.3 15.0 %collective-permute-start.15 = (f32[2,2,4,1,128]{4,2,1,0,3:T(4,128)S(1)}, f32[2,2,4,1,128]{4,2,1,0,3:T(4,128)S(1)}, u32[]{:S(2)}, u32[]{:S(2)}) collective-permute-start(f32[2,2,4,1,128]{4,2,1,0,3:T(4,128)S(1)} %get-tuple-element.35), channel_id=1, source_target_pairs={{1,0},{2,1},{3,2},{4,3},{5,4},{6,5},{7,6},{8,7},{9,8},{10,9},{11,1... | collective-permute-start | bytes 24584 | tf_op jit(solution)/shard_map/ppermute | solution.py:30
  82.7 4.9 %collective-permute-start.18 = (f32[2,2,4,1,128]{4,0,2,1,3:T(2,128)S(1)}, f32[2,2,4,1,128]{4,0,2,1,3:T(2,128)S(1)}, u32[]{:S(2)}, u32[]{:S(2)}) collective-permute-start(f32[2,2,4,1,128]{4,0,2,1,3:T(2,128)S(1)} %fusion.300), channel_id=1, source_target_pairs={{0,1},{1,2},{2,3},{3,4},{4,5},{5,6},{6,7},{7,8},{8,9},{9,10},{10,1... | collective-permute-start | bytes 24584 | tf_op jit(solution)/shard_map/ppermute | solution.py:28
  87.7 8.2 %collective-permute-start.19 = (f32[2,2,4,1,128]{4,0,2,1,3:T(2,128)S(1)}, f32[2,2,4,1,128]{4,0,2,1,3:T(2,128)S(1)}, u32[]{:S(2)}, u32[]{:S(2)}) collective-permute-start(f32[2,2,4,1,128]{4,0,2,1,3:T(2,128)S(1)} %get-tuple-element.37), channel_id=1, source_target_pairs={{1,0},{2,1},{3,2},{4,3},{5,4},{6,5},{7,6},{8,7},{9,8},{10,9},{11,1... | collective-permute-start | bytes 24584 | tf_op jit(solution)/shard_map/ppermute | solution.py:30
  110.2 8.2 %collective-permute-start.23 = (f32[2,2,4,1,128]{4,2,1,0,3:T(4,128)S(1)}, f32[2,2,4,1,128]{4,2,1,0,3:T(4,128)S(1)}, u32[]{:S(2)}, u32[]{:S(2)}) collective-permute-start(f32[2,2,4,1,128]{4,2,1,0,3:T(4,128)S(1)} %get-tuple-element.33), channel_id=1, source_target_pairs={{1,0},{2,1},{3,2},{4,3},{5,4},{6,5},{7,6},{8,7},{9,8},{10,9},{11,1... | collective-permute-start | bytes 24584 | tf_op jit(solution)/shard_map/ppermute | solution.py:30
  127.0 4.7 %collective-permute-start.26 = (f32[2,2,4,1,128]{4,2,1,0,3:T(4,128)S(1)}, f32[2,2,4,1,128]{4,2,1,0,3:T(4,128)S(1)}, u32[]{:S(2)}, u32[]{:S(2)}) collective-permute-start(f32[2,2,4,1,128]{4,2,1,0,3:T(4,128)S(1)} %fusion.297), channel_id=1, source_target_pairs={{0,1},{1,2},{2,3},{3,4},{4,5},{5,6},{6,7},{7,8},{8,9},{9,10},{10,1... | collective-permute-start | bytes 24584 | tf_op jit(solution)/shard_map/ppermute | solution.py:28
  131.7 8.2 %collective-permute-start.27 = (f32[2,2,4,1,128]{4,2,1,0,3:T(4,128)S(1)}, f32[2,2,4,1,128]{4,2,1,0,3:T(4,128)S(1)}, u32[]{:S(2)}, u32[]{:S(2)}) collective-permute-start(f32[2,2,4,1,128]{4,2,1,0,3:T(4,128)S(1)} %get-tuple-element.31), channel_id=1, source_target_pairs={{1,0},{2,1},{3,2},{4,3},{5,4},{6,5},{7,6},{8,7},{9,8},{10,9},{11,1... | collective-permute-start | bytes 24584 | tf_op jit(solution)/shard_map/ppermute | solution.py:30
  148.5 4.7 %collective-permute-start.30 = (f32[2,2,4,1,128]{4,2,1,0,3:T(4,128)S(1)}, f32[2,2,4,1,128]{4,2,1,0,3:T(4,128)S(1)}, u32[]{:S(2)}, u32[]{:S(2)}) collective-permute-start(f32[2,2,4,1,128]{4,2,1,0,3:T(4,128)S(1)} %fusion.295), channel_id=1, source_target_pairs={{0,1},{1,2},{2,3},{3,4},{4,5},{5,6},{6,7},{7,8},{8,9},{9,10},{10,1... | collective-permute-start | bytes 24584 | tf_op jit(solution)/shard_map/ppermute | solution.py:28
  153.2 8.2 %collective-permute-start.31 = (f32[2,2,4,1,128]{4,2,1,0,3:T(4,128)S(1)}, f32[2,2,4,1,128]{4,2,1,0,3:T(4,128)S(1)}, u32[]{:S(2)}, u32[]{:S(2)}) collective-permute-start(f32[2,2,4,1,128]{4,2,1,0,3:T(4,128)S(1)} %get-tuple-element.29), channel_id=1, source_target_pairs={{1,0},{2,1},{3,2},{4,3},{5,4},{6,5},{7,6},{8,7},{9,8},{10,9},{11,1... | collective-permute-start | bytes 24584 | tf_op jit(solution)/shard_map/ppermute | solution.py:30
  170.6 4.9 %collective-permute-start.33 = (f32[5,5,4,1,1]{4,2,0,1,3:T(4,128)S(1)}, f32[5,5,4,1,1]{4,2,0,1,3:T(4,128)S(1)}, u32[]{:S(2)}, u32[]{:S(2)}) collective-permute-start(f32[5,5,4,1,1]{4,2,0,1,3:T(4,128)S(1)} %get-tuple-element.135), channel_id=1, source_target_pairs={{16,0},{17,1},{18,2},{19,3},{20,4},{21,5},{22,6},{23,7},{24,8},{25... | collective-permute-start | bytes 1208 | tf_op jit(solution)/shard_map/ppermute | solution.py:30
  175.7 5.1 %collective-permute-start.34 = (f32[5,5,4,1,128]{4,2,1,0,3:T(4,128)S(1)}, f32[5,5,4,1,128]{4,2,1,0,3:T(4,128)S(1)}, u32[]{:S(2)}, u32[]{:S(2)}) collective-permute-start(f32[5,5,4,1,128]{4,2,1,0,3:T(4,128)S(1)} %maximum_bitcast_fusion.24), channel_id=1, source_target_pairs={{0,1},{1,2},{2,3},{3,4},{4,5},{5,6},{6,7},{7,8},{8,9},{9,10},{10,1... | collective-permute-start | bytes 153608 | tf_op jit(solution)/shard_map/ppermute | solution.py:28
  180.9 8.7 %collective-permute-start.35 = (f32[5,5,4,1,128]{4,2,1,0,3:T(4,128)S(1)}, f32[5,5,4,1,128]{4,2,1,0,3:T(4,128)S(1)}, u32[]{:S(2)}, u32[]{:S(2)}) collective-permute-start(f32[5,5,4,1,128]{4,2,1,0,3:T(4,128)S(1)} %get-tuple-element.27), channel_id=1, source_target_pairs={{1,0},{2,1},{3,2},{4,3},{5,4},{6,5},{7,6},{8,7},{9,8},{10,9},{11,1... | collective-permute-start | bytes 153608 | tf_op jit(solution)/shard_map/ppermute | solution.py:30
  197.8 4.9 %collective-permute-start.37 = (f32[5,5,4,1,1]{4,2,0,1,3:T(4,128)S(1)}, f32[5,5,4,1,1]{4,2,0,1,3:T(4,128)S(1)}, u32[]{:S(2)}, u32[]{:S(2)}) collective-permute-start(f32[5,5,4,1,1]{4,2,0,1,3:T(4,128)S(1)} %get-tuple-element.129), channel_id=1, source_target_pairs={{16,0},{17,1},{18,2},{19,3},{20,4},{21,5},{22,6},{23,7},{24,8},{25... | collective-permute-start | bytes 1208 | tf_op jit(solution)/shard_map/ppermute | solution.py:30
  202.9 5.1 %collective-permute-start.38 = (f32[5,5,4,1,128]{4,2,1,0,3:T(4,128)S(1)}, f32[5,5,4,1,128]{4,2,1,0,3:T(4,128)S(1)}, u32[]{:S(2)}, u32[]{:S(2)}) collective-permute-start(f32[5,5,4,1,128]{4,2,1,0,3:T(4,128)S(1)} %maximum_bitcast_fusion.20), channel_id=1, source_target_pairs={{0,1},{1,2},{2,3},{3,4},{4,5},{5,6},{6,7},{7,8},{8,9},{9,10},{10,1... | collective-permute-start | bytes 153608 | tf_op jit(solution)/shard_map/ppermute | solution.py:28
  208.0 8.7 %collective-permute-start.39 = (f32[5,5,4,1,128]{4,2,1,0,3:T(4,128)S(1)}, f32[5,5,4,1,128]{4,2,1,0,3:T(4,128)S(1)}, u32[]{:S(2)}, u32[]{:S(2)}) collective-permute-start(f32[5,5,4,1,128]{4,2,1,0,3:T(4,128)S(1)} %get-tuple-element.25), channel_id=1, source_target_pairs={{1,0},{2,1},{3,2},{4,3},{5,4},{6,5},{7,6},{8,7},{9,8},{10,9},{11,1... | collective-permute-start | bytes 153608 | tf_op jit(solution)/shard_map/ppermute | solution.py:30
  224.9 4.9 %collective-permute-start.41 = (f32[5,5,4,1,1]{4,2,0,1,3:T(4,128)S(1)}, f32[5,5,4,1,1]{4,2,0,1,3:T(4,128)S(1)}, u32[]{:S(2)}, u32[]{:S(2)}) collective-permute-start(f32[5,5,4,1,1]{4,2,0,1,3:T(4,128)S(1)} %get-tuple-element.123), channel_id=1, source_target_pairs={{16,0},{17,1},{18,2},{19,3},{20,4},{21,5},{22,6},{23,7},{24,8},{25... | collective-permute-start | bytes 1208 | tf_op jit(solution)/shard_map/ppermute | solution.py:30
  230.0 5.1 %collective-permute-start.42 = (f32[5,5,4,1,128]{4,2,1,0,3:T(4,128)S(1)}, f32[5,5,4,1,128]{4,2,1,0,3:T(4,128)S(1)}, u32[]{:S(2)}, u32[]{:S(2)}) collective-permute-start(f32[5,5,4,1,128]{4,2,1,0,3:T(4,128)S(1)} %maximum_bitcast_fusion.16), channel_id=1, source_target_pairs={{0,1},{1,2},{2,3},{3,4},{4,5},{5,6},{6,7},{7,8},{8,9},{9,10},{10,1... | collective-permute-start | bytes 153608 | tf_op jit(solution)/shard_map/ppermute | solution.py:28
  235.1 8.7 %collective-permute-start.43 = (f32[5,5,4,1,128]{4,2,1,0,3:T(4,128)S(1)}, f32[5,5,4,1,128]{4,2,1,0,3:T(4,128)S(1)}, u32[]{:S(2)}, u32[]{:S(2)}) collective-permute-start(f32[5,5,4,1,128]{4,2,1,0,3:T(4,128)S(1)} %get-tuple-element.23), channel_id=1, source_target_pairs={{1,0},{2,1},{3,2},{4,3},{5,4},{6,5},{7,6},{8,7},{9,8},{10,9},{11,1... | collective-permute-start | bytes 153608 | tf_op jit(solution)/shard_map/ppermute | solution.py:30
  252.1 4.9 %collective-permute-start.45 = (f32[5,5,4,1,1]{4,2,0,1,3:T(4,128)S(1)}, f32[5,5,4,1,1]{4,2,0,1,3:T(4,128)S(1)}, u32[]{:S(2)}, u32[]{:S(2)}) collective-permute-start(f32[5,5,4,1,1]{4,2,0,1,3:T(4,128)S(1)} %get-tuple-element.117), channel_id=1, source_target_pairs={{16,0},{17,1},{18,2},{19,3},{20,4},{21,5},{22,6},{23,7},{24,8},{25... | collective-permute-start | bytes 1208 | tf_op jit(solution)/shard_map/ppermute | solution.py:30
  257.2 5.1 %collective-permute-start.46 = (f32[5,5,4,1,128]{4,2,1,0,3:T(4,128)S(1)}, f32[5,5,4,1,128]{4,2,1,0,3:T(4,128)S(1)}, u32[]{:S(2)}, u32[]{:S(2)}) collective-permute-start(f32[5,5,4,1,128]{4,2,1,0,3:T(4,128)S(1)} %maximum_bitcast_fusion.12), channel_id=1, source_target_pairs={{0,1},{1,2},{2,3},{3,4},{4,5},{5,6},{6,7},{7,8},{8,9},{9,10},{10,1... | collective-permute-start | bytes 153608 | tf_op jit(solution)/shard_map/ppermute | solution.py:28
  262.2 8.7 %collective-permute-start.47 = (f32[5,5,4,1,128]{4,2,1,0,3:T(4,128)S(1)}, f32[5,5,4,1,128]{4,2,1,0,3:T(4,128)S(1)}, u32[]{:S(2)}, u32[]{:S(2)}) collective-permute-start(f32[5,5,4,1,128]{4,2,1,0,3:T(4,128)S(1)} %get-tuple-element.21), channel_id=1, source_target_pairs={{1,0},{2,1},{3,2},{4,3},{5,4},{6,5},{7,6},{8,7},{9,8},{10,9},{11,1... | collective-permute-start | bytes 153608 | tf_op jit(solution)/shard_map/ppermute | solution.py:30
  288.9 8.2 %collective-permute-start.51 = (f32[2,2,4,1,128]{4,2,1,0,3:T(4,128)S(1)}, f32[2,2,4,1,128]{4,2,1,0,3:T(4,128)S(1)}, u32[]{:S(2)}, u32[]{:S(2)}) collective-permute-start(f32[2,2,4,1,128]{4,2,1,0,3:T(4,128)S(1)} %get-tuple-element.19), channel_id=1, source_target_pairs={{1,0},{2,1},{3,2},{4,3},{5,4},{6,5},{7,6},{8,7},{9,8},{10,9},{11,1... | collective-permute-start | bytes 24584 | tf_op jit(solution)/shard_map/ppermute | solution.py:30
  305.6 4.7 %collective-permute-start.54 = (f32[2,2,4,1,128]{4,2,1,0,3:T(4,128)S(1)}, f32[2,2,4,1,128]{4,2,1,0,3:T(4,128)S(1)}, u32[]{:S(2)}, u32[]{:S(2)}) collective-permute-start(f32[2,2,4,1,128]{4,2,1,0,3:T(4,128)S(1)} %fusion.291), channel_id=1, source_target_pairs={{0,1},{1,2},{2,3},{3,4},{4,5},{5,6},{6,7},{7,8},{8,9},{9,10},{10,1... | collective-permute-start | bytes 24584 | tf_op jit(solution)/shard_map/ppermute | solution.py:28
  310.4 8.2 %collective-permute-start.55 = (f32[2,2,4,1,128]{4,2,1,0,3:T(4,128)S(1)}, f32[2,2,4,1,128]{4,2,1,0,3:T(4,128)S(1)}, u32[]{:S(2)}, u32[]{:S(2)}) collective-permute-start(f32[2,2,4,1,128]{4,2,1,0,3:T(4,128)S(1)} %get-tuple-element.17), channel_id=1, source_target_pairs={{1,0},{2,1},{3,2},{4,3},{5,4},{6,5},{7,6},{8,7},{9,8},{10,9},{11,1... | collective-permute-start | bytes 24584 | tf_op jit(solution)/shard_map/ppermute | solution.py:30
  327.1 4.7 %collective-permute-start.58 = (f32[2,2,4,1,128]{4,2,1,0,3:T(4,128)S(1)}, f32[2,2,4,1,128]{4,2,1,0,3:T(4,128)S(1)}, u32[]{:S(2)}, u32[]{:S(2)}) collective-permute-start(f32[2,2,4,1,128]{4,2,1,0,3:T(4,128)S(1)} %fusion.289), channel_id=1, source_target_pairs={{0,1},{1,2},{2,3},{3,4},{4,5},{5,6},{6,7},{7,8},{8,9},{9,10},{10,1... | collective-permute-start | bytes 24584 | tf_op jit(solution)/shard_map/ppermute | solution.py:28
  331.8 8.2 %collective-permute-start.59 = (f32[2,2,4,1,128]{4,2,1,0,3:T(4,128)S(1)}, f32[2,2,4,1,128]{4,2,1,0,3:T(4,128)S(1)}, u32[]{:S(2)}, u32[]{:S(2)}) collective-permute-start(f32[2,2,4,1,128]{4,2,1,0,3:T(4,128)S(1)} %get-tuple-element.15), channel_id=1, source_target_pairs={{1,0},{2,1},{3,2},{4,3},{5,4},{6,5},{7,6},{8,7},{9,8},{10,9},{11,1... | collective-permute-start | bytes 24584 | tf_op jit(solution)/shard_map/ppermute | solution.py:30
  348.6 4.7 %collective-permute-start.62 = (f32[2,2,4,1,128]{4,2,0,1,3:T(4,128)S(1)}, f32[2,2,4,1,128]{4,2,0,1,3:T(4,128)S(1)}, u32[]{:S(2)}, u32[]{:S(2)}) collective-permute-start(f32[2,2,4,1,128]{4,2,0,1,3:T(4,128)S(1)} %fusion.287), channel_id=1, source_target_pairs={{0,1},{1,2},{2,3},{3,4},{4,5},{5,6},{6,7},{7,8},{8,9},{9,10},{10,1... | collective-permute-start | bytes 24584 | tf_op jit(solution)/shard_map/ppermute | solution.py:28
  353.3 8.2 %collective-permute-start.63 = (f32[2,2,4,1,128]{4,2,0,1,3:T(4,128)S(1)}, f32[2,2,4,1,128]{4,2,0,1,3:T(4,128)S(1)}, u32[]{:S(2)}, u32[]{:S(2)}) collective-permute-start(f32[2,2,4,1,128]{4,2,0,1,3:T(4,128)S(1)} %get-tuple-element.13), channel_id=1, source_target_pairs={{1,0},{2,1},{3,2},{4,3},{5,4},{6,5},{7,6},{8,7},{9,8},{10,9},{11,1... | collective-permute-start | bytes 24584 | tf_op jit(solution)/shard_map/ppermute | solution.py:30
  370.7 4.9 %collective-permute-start.65 = (f32[5,5,4,1,1]{4,2,0,1,3:T(4,128)S(1)}, f32[5,5,4,1,1]{4,2,0,1,3:T(4,128)S(1)}, u32[]{:S(2)}, u32[]{:S(2)}) collective-permute-start(f32[5,5,4,1,1]{4,2,0,1,3:T(4,128)S(1)} %get-tuple-element.111), channel_id=1, source_target_pairs={{16,0},{17,1},{18,2},{19,3},{20,4},{21,5},{22,6},{23,7},{24,8},{25... | collective-permute-start | bytes 1208 | tf_op jit(solution)/shard_map/ppermute | solution.py:30
  375.8 5.1 %collective-permute-start.66 = (f32[5,5,4,1,128]{4,2,0,1,3:T(4,128)S(1)}, f32[5,5,4,1,128]{4,2,0,1,3:T(4,128)S(1)}, u32[]{:S(2)}, u32[]{:S(2)}) collective-permute-start(f32[5,5,4,1,128]{4,2,0,1,3:T(4,128)S(1)} %maximum_bitcast_fusion.8), channel_id=1, source_target_pairs={{0,1},{1,2},{2,3},{3,4},{4,5},{5,6},{6,7},{7,8},{8,9},{9,10},{10,1... | collective-permute-start | bytes 153608 | tf_op jit(solution)/shard_map/ppermute | solution.py:28
  381.0 8.7 %collective-permute-start.67 = (f32[5,5,4,1,128]{4,2,0,1,3:T(4,128)S(1)}, f32[5,5,4,1,128]{4,2,0,1,3:T(4,128)S(1)}, u32[]{:S(2)}, u32[]{:S(2)}) collective-permute-start(f32[5,5,4,1,128]{4,2,0,1,3:T(4,128)S(1)} %get-tuple-element.11), channel_id=1, source_target_pairs={{1,0},{2,1},{3,2},{4,3},{5,4},{6,5},{7,6},{8,7},{9,8},{10,9},{11,1... | collective-permute-start | bytes 153608 | tf_op jit(solution)/shard_map/ppermute | solution.py:30
  398.0 4.9 %collective-permute-start.69 = (f32[5,5,4,1,1]{4,2,0,1,3:T(4,128)S(1)}, f32[5,5,4,1,1]{4,2,0,1,3:T(4,128)S(1)}, u32[]{:S(2)}, u32[]{:S(2)}) collective-permute-start(f32[5,5,4,1,1]{4,2,0,1,3:T(4,128)S(1)} %get-tuple-element.105), channel_id=1, source_target_pairs={{16,0},{17,1},{18,2},{19,3},{20,4},{21,5},{22,6},{23,7},{24,8},{25... | collective-permute-start | bytes 1208 | tf_op jit(solution)/shard_map/ppermute | solution.py:30
  403.1 5.1 %collective-permute-start.70 = (f32[5,5,4,1,128]{4,2,1,0,3:T(4,128)S(1)}, f32[5,5,4,1,128]{4,2,1,0,3:T(4,128)S(1)}, u32[]{:S(2)}, u32[]{:S(2)}) collective-permute-start(f32[5,5,4,1,128]{4,2,1,0,3:T(4,128)S(1)} %maximum_bitcast_fusion.6), channel_id=1, source_target_pairs={{0,1},{1,2},{2,3},{3,4},{4,5},{5,6},{6,7},{7,8},{8,9},{9,10},{10,1... | collective-permute-start | bytes 153608 | tf_op jit(solution)/shard_map/ppermute | solution.py:28
  408.2 8.7 %collective-permute-start.71 = (f32[5,5,4,1,128]{4,2,1,0,3:T(4,128)S(1)}, f32[5,5,4,1,128]{4,2,1,0,3:T(4,128)S(1)}, u32[]{:S(2)}, u32[]{:S(2)}) collective-permute-start(f32[5,5,4,1,128]{4,2,1,0,3:T(4,128)S(1)} %get-tuple-element.9), channel_id=1, source_target_pairs={{1,0},{2,1},{3,2},{4,3},{5,4},{6,5},{7,6},{8,7},{9,8},{10,9},{11,1... | collective-permute-start | bytes 153608 | tf_op jit(solution)/shard_map/ppermute | solution.py:30
  425.2 4.9 %collective-permute-start.73 = (f32[5,5,4,1,1]{4,2,0,1,3:T(4,128)S(1)}, f32[5,5,4,1,1]{4,2,0,1,3:T(4,128)S(1)}, u32[]{:S(2)}, u32[]{:S(2)}) collective-permute-start(f32[5,5,4,1,1]{4,2,0,1,3:T(4,128)S(1)} %get-tuple-element.99), channel_id=1, source_target_pairs={{16,0},{17,1},{18,2},{19,3},{20,4},{21,5},{22,6},{23,7},{24,8},{25... | collective-permute-start | bytes 1208 | tf_op jit(solution)/shard_map/ppermute | solution.py:30
  430.3 5.1 %collective-permute-start.74 = (f32[5,5,4,1,128]{4,2,0,1,3:T(4,128)S(1)}, f32[5,5,4,1,128]{4,2,0,1,3:T(4,128)S(1)}, u32[]{:S(2)}, u32[]{:S(2)}) collective-permute-start(f32[5,5,4,1,128]{4,2,0,1,3:T(4,128)S(1)} %maximum_bitcast_fusion.2), channel_id=1, source_target_pairs={{0,1},{1,2},{2,3},{3,4},{4,5},{5,6},{6,7},{7,8},{8,9},{9,10},{10,1... | collective-permute-start | bytes 153608 | tf_op jit(solution)/shard_map/ppermute | solution.py:28
  435.4 8.7 %collective-permute-start.75 = (f32[5,5,4,1,128]{4,2,0,1,3:T(4,128)S(1)}, f32[5,5,4,1,128]{4,2,0,1,3:T(4,128)S(1)}, u32[]{:S(2)}, u32[]{:S(2)}) collective-permute-start(f32[5,5,4,1,128]{4,2,0,1,3:T(4,128)S(1)} %get-tuple-element.7), channel_id=1, source_target_pairs={{1,0},{2,1},{3,2},{4,3},{5,4},{6,5},{7,6},{8,7},{9,8},{10,9},{11,1... | collective-permute-start | bytes 153608 | tf_op jit(solution)/shard_map/ppermute | solution.py:30
  (56 other events, 226.6 us)
where the time goes:
time: 455 us; the launch traced here: 447 us
  waiting for transfers between devices  191 us (42%)
  starting transfers between devices  164 us (36%)
  matrix products  62 us (14%)
  other arithmetic  12.6 us (3%)
  local copies, waits for them, and re-layouts  12.5 us (3%)
  between operations  4.75 us (1%)
    ppermute x38, waiting for transfers between devices, padded_2(): lax.ppermute(head, axis, [((i + 1) % count, i) for i in range(ends)])  162 us
    ppermute x38, starting transfers between devices, padded_2(): lax.ppermute(tail, axis, [(i, (i + 1) % count) for i in range(ends)])  99.9 us
    ppermute x38, starting transfers between devices, padded_2(): lax.ppermute(head, axis, [((i + 1) % count, i) for i in range(ends)])  64.5 us
    ppermute x38, waiting for transfers between devices, padded_2(): lax.ppermute(tail, axis, [(i, (i + 1) % count) for i in range(ends)])  28.8 us
    dot_general x52, matrix products, along(): jnp.einsum('pa,a...->p...', matrix, field, precision=lax.Precision.HIGHEST)  23.3 us
    dot_general x52, matrix products, along(): jnp.einsum('qb,ab...->aq...', matrix, field, precision=lax.Precision.HIGH...  23 us
    dot_general x36, matrix products, along(): jnp.einsum('rc,abc...->abr...', matrix, field, precision=lax.Precision.HI...  15.7 us
  transfers between devices with their start and end apart: 76, of which 66 were waited for; matrix products, arithmetic and copies ran while one was open for 3% of the time, Pallas kernels for 0%

commit v1 on v0

v1 whole, which is shorter than its diff:
```python
import functools
import math

import jax
import jax.numpy as jnp
import numpy as np
from jax import lax
from jax.experimental import pallas as pl
from jax.experimental.pallas import tpu as pltpu
from jax.sharding import PartitionSpec as P

N = 5
CYCLES = 2
NPRE = 2
NPOST = 2
NC = 4
FINE_RELAX = 0.25
COARSE_RELAX = 0.4
REACH = NC
STEPS = CYCLES * (NPRE + NPOST) + 1
HALO = 32
MESH = pl.DeviceIdType.MESH
F32 = jnp.float32


def node_tables():
    points = np.array([-1.0, -math.sqrt(3.0 / 7.0), 0.0, math.sqrt(3.0 / 7.0), 1.0])
    weights = np.array([0.1, 49.0 / 90.0, 32.0 / 45.0, 49.0 / 90.0, 0.1])
    eye_table = np.eye(points.shape[0])
    spread = points[:, None] - points[None, :] + eye_table
    factors = np.prod(spread, axis=1)
    deriv = factors[:, None] / (factors[None, :] * spread)
    deriv = np.where(eye_table > 0, (np.sum(1.0 / spread, axis=1) - 1.0)[:, None], deriv)
    stiff = deriv.T @ (weights[:, None] * deriv)
    mass = eye_table * weights[:, None]
    interp = np.stack([(1.0 - points) / 2.0, (1.0 + points) / 2.0], axis=1)
    return stiff, weights, interp, interp.T @ stiff @ interp, interp.T @ mass @ interp


STIFF, WEIGHTS, INTERP, COARSE_STIFF, COARSE_MASS = node_tables()
D = STIFF / WEIGHTS[:, None]
W3 = WEIGHTS[:, None, None] * WEIGHTS[None, :, None] * WEIGHTS[None, None, :]
DD = np.diag(D)
K3 = W3 * (DD[:, None, None] + DD[None, :, None] + DD[None, None, :])


def node(a, b, c):
    return (a * N + b) * N + c


def line_parts(v):
    twice = v[2] + v[2]
    return (v[0] + v[4]) - twice, (v[1] + v[3]) - twice, v[0] - v[4], v[1] - v[3]


def row_even(i, parts):
    return float((D[i, 0] + D[i, 4]) / 2) * parts[0] + float((D[i, 1] + D[i, 3]) / 2) * parts[1]


def row_odd(i, parts):
    return float((D[i, 0] - D[i, 4]) / 2) * parts[2] + float((D[i, 1] - D[i, 3]) / 2) * parts[3]


def line_apply(v):
    parts = line_parts(v)
    e0, e1, e2 = (row_even(i, parts) for i in range(3))
    o0, o1 = (row_odd(i, parts) for i in range(2))
    return [e0 + o0, e1 + o1, e2, e1 - o1, e0 - o0]


def scaled(factor, value):
    factor = float(factor)
    if factor == 1.0:
        return value
    return factor * value


def mix(pairs):
    total = None
    for factor, value in pairs:
        if abs(float(factor)) < 1e-14:
            continue
        term = scaled(factor, value)
        total = term if total is None else total + term
    return total


def kernel(
    sizes, load_ref, kappa_ref, wet_ref, sol_out, res_out,
    other_load, other_coeff, own_coeff, load, coeffs, sol, total, inverse, cinv, face, got, cgot,
    ex_send, ex_recv, k_send, k_recv, f_send, f_recv, c_send, c_recv,
):
    ex_count, ey_count, lin_count, layers, width = sizes
    ex, ey, lin = lax.axis_index("ex"), lax.axis_index("ey"), lax.axis_index("lin")
    rows = ey_count * lin_count
    row = ey * lin_count + lin
    own = REACH

    sub = lax.broadcasted_iota(jnp.int32, (2 * layers, width), 0)
    lane = lax.broadcasted_iota(jnp.int32, (2 * layers, width), 1)
    layer = sub % layers
    bottom, top = layer == 0, layer == layers - 1
    first_lane, last_lane = lane == 0, lane == width - 1
    near = jnp.where(ex == 0, lane, width - 1 - lane)
    real = (sub < layers) | (near < HALO)

    def like(mask, x):
        return jnp.broadcast_to(mask, x.shape) if x.ndim == 3 else mask

    def before(x):
        y = pltpu.roll(x, 1, x.ndim - 1)
        return jnp.where(like(first_lane, x), pltpu.roll(y, layers, x.ndim - 2), y)

    def after(x):
        y = pltpu.roll(x, width - 1, x.ndim - 1)
        return jnp.where(like(last_lane, x), pltpu.roll(y, layers, x.ndim - 2), y)

    def below(low, high):
        return jnp.where(like(bottom, low), low, low + pltpu.roll(high, 1, low.ndim - 2))

    def above(low):
        return jnp.where(like(top, low), 0.0, pltpu.roll(low, 2 * layers - 1, low.ndim - 2))

    def place(at):
        return (ex, at // lin_count, at % lin_count)

    def partners(fn):
        for d in range(1, REACH + 1):
            @pl.when(row >= d)
            def _():
                fn(row - d, own + d, own - d)

            @pl.when(row + d < rows)
            def _():
                fn(row + d, own - d, own + d)

    coeffs[...] = jnp.zeros_like(coeffs)
    cgot[...] = jnp.zeros_like(cgot)
    got[...] = jnp.zeros_like(got)
    barrier = pltpu.get_barrier_semaphore()
    pl.semaphore_signal(barrier, inc=1, device_id=(1 - ex, ey, lin), device_id_type=MESH)
    partners(lambda at, theirs, mine: pl.semaphore_signal(
        barrier, inc=1, device_id=place(at), device_id_type=MESH))

    coeff_own = kappa_ref[...] * jnp.where(wet_ref[...] == 1, F32(1.0), F32(0.05))
    own_coeff[...] = coeff_own

    pl.semaphore_wait(barrier, 1 + jnp.minimum(row, REACH) + jnp.minimum(rows - 1 - row, REACH))

    def ex_copy(src, dst, i):
        return pltpu.make_async_remote_copy(
            src_ref=src, dst_ref=dst, send_sem=ex_send.at[i], recv_sem=ex_recv.at[i],
            device_id=(1 - ex, ey, lin), device_id_type=MESH)

    coeff_copy = ex_copy(own_coeff, other_coeff, 0)
    load_copy = ex_copy(load_ref, other_load, 1)
    coeff_copy.start()
    load_copy.start()
    sol[...] = jnp.zeros_like(sol)
    coeff_copy.wait()
    coeffs[own] = jnp.where(real, jnp.concatenate([coeff_own, other_coeff[...]], axis=0), 0.0)

    def k_copy(at, theirs, mine):
        return pltpu.make_async_remote_copy(
            src_ref=coeffs.at[own], dst_ref=coeffs.at[theirs],
            send_sem=k_send.at[mine], recv_sem=k_recv.at[theirs],
            device_id=place(at), device_id_type=MESH)

    def k_wait(at, theirs, mine):
        pltpu.make_async_remote_copy(
            src_ref=coeffs.at[own], dst_ref=coeffs.at[mine],
            send_sem=k_send.at[mine], recv_sem=k_recv.at[mine],
            device_id=place(at), device_id_type=MESH).wait()

    partners(lambda *p: k_copy(*p).start())
    load_copy.wait()

    def join(i, _):
        load[i] = jnp.where(real, jnp.concatenate([load_ref[i], other_load[i]], axis=0), 0.0)
        return 0

    lax.fori_loop(0, N * N * N, join, 0)
    partners(k_wait)

    def inverted(x):
        return jnp.where(x > 0.0, 1.0 / jnp.where(x > 0.0, x, 1.0), 0.0)

    here = coeffs[own]
    for kind, x in enumerate((here, here + coeffs[own - 1], here + coeffs[own + 1])):
        xc = x + before(x)
        for slot, y in enumerate((x, xc, below(x, x), below(xc, xc))):
            inverse[kind * 4 + slot] = inverted(y)
    pairs = coeffs[0:2 * REACH] + coeffs[1:2 * REACH + 1]
    pairs = pairs + before(pairs)
    pairs = below(pairs, pairs)
    corner = 3.0 * COARSE_STIFF[0, 0] * COARSE_MASS[0, 0] ** 2
    cinv[...] = float(COARSE_RELAX / corner) * inverted(pairs)

    def plane_local(b):
        v = [[sol[node(a, b, c)] for c in range(N)] for a in range(N)]
        acc = [line_apply(v[a]) for a in range(N)]
        for c in range(N):
            column = line_apply([v[a][c] for a in range(N)])
            for a in range(N):
                acc[a][c] = acc[a][c] + column[a]
        coeff = coeffs[own]
        out = []
        for a in range(N):
            line = []
            for c in range(N):
                parts = line_parts([sol[node(a, k, c)] for k in range(N)])
                side = min(b, N - 1 - b)
                term = row_even(side, parts)
                if b < 2:
                    term = term + row_odd(side, parts)
                elif b > 2:
                    term = term - row_odd(side, parts)
                value = acc[a][c] + term
                line.append(load[node(a, b, c)] - float(W3[a, b, c]) * coeff * value)
            out.append(line)
        return out

    def gather_plane(f):
        h = []
        for a in range(N):
            h.append([f[a][0] + before(f[a][N - 1])] + f[a][1:N - 1])
        return [[below(h[0][c], h[N - 1][c]) for c in range(N - 1)]] + h[1:N - 1]

    def put_plane(b, values, ref):
        for a in range(N - 1):
            line = list(values[a])
            line.append(after(line[0]))
            for c in range(N):
                ref[node(a, b, c)] = line[c]
                if a == 0:
                    ref[node(N - 1, b, c)] = above(line[c])

    def update_plane(b, scale):
        kind = 0 if 0 < b < N - 1 else (1 if b == 0 else 2)
        values = []
        for a in range(N - 1):
            line = []
            for c in range(N - 1):
                inv = inverse[kind * 4 + (2 if a == 0 else 0) + (1 if c == 0 else 0)] * scale
                line.append(sol[node(a, b, c)] + float(FINE_RELAX / K3[a, b, c]) * inv * total[(b * 4 + a) * 4 + c])
            values.append(line)
        put_plane(b, values, sol)

    def c_copy(cycle, at, theirs, mine):
        return pltpu.make_async_remote_copy(
            src_ref=cgot.at[cycle, own], dst_ref=cgot.at[cycle, theirs],
            send_sem=c_send.at[mine], recv_sem=c_recv.at[cycle, theirs],
            device_id=place(at), device_id_type=MESH)

    def c_wait(cycle, at, theirs, mine):
        pltpu.make_async_remote_copy(
            src_ref=cgot.at[cycle, own], dst_ref=cgot.at[cycle, mine],
            send_sem=c_send.at[mine], recv_sem=c_recv.at[cycle, mine],
            device_id=place(at), device_id_type=MESH).wait()

    def coarse(cycle):
        q = {}
        for b in range(N):
            f = plane_local(b)
            g = [[mix((INTERP[c, k], f[a][c]) for c in range(N)) for k in range(2)] for a in range(N)]
            for i in range(2):
                for k in range(2):
                    h = mix((INTERP[a, i], g[a][k]) for a in range(N))
                    for j in range(2):
                        if INTERP[b, j] != 0:
                            term = scaled(INTERP[b, j], h)
                            q[i, j, k] = q[i, j, k] + term if (i, j, k) in q else term

        def gather(q, j):
            h = [q[i, j, 0] + before(q[i, j, 1]) for i in range(2)]
            return below(h[0], h[1])

        for j in range(2):
            cgot[cycle, own, j] = gather(q, j)
        partners(lambda *p: c_copy(cycle, *p).start())
        partners(lambda *p: c_wait(cycle, *p))
        lines = 2 * REACH
        rc = cgot[cycle, 0:lines, 1] + cgot[cycle, 1:lines + 1, 0]
        inv = cinv[...]
        correction = inv * rc
        coeff = coeffs[1:lines]

        def corners(x):
            right = after(x)
            return {(0, 0): x, (0, 1): right, (1, 0): above(x), (1, 1): above(right)}

        def two(m, x, y):
            return [mix(((m[p, 0], x), (m[p, 1], y))) for p in range(2)]

        for sweep in range(NC - 1):
            nodes = corners(correction)
            v = {(i, j, k): nodes[i, k][j:j + lines - 1] for i in range(2) for j in range(2) for k in range(2)}

            def along(m, v, axis):
                out = {}
                for x in range(2):
                    for y in range(2):
                        key = [(0, x, y), (x, 0, y), (x, y, 0)][axis]
                        key1 = [(1, x, y), (x, 1, y), (x, y, 1)][axis]
                        out[key], out[key1] = two(m, v[key], v[key1])
                return out

            mc = along(COARSE_MASS, v, 2)
            first = along(COARSE_STIFF, along(COARSE_MASS, mc, 1), 0)
            rest = along(COARSE_STIFF, mc, 1)
            third = along(COARSE_MASS, along(COARSE_STIFF, v, 2), 1)
            rest = along(COARSE_MASS, {key: rest[key] + third[key] for key in rest}, 0)
            q2 = {key: coeff * (first[key] + rest[key]) for key in rest}
            low, high = gather(q2, 0), gather(q2, 1)
            zero = jnp.zeros_like(low[0:1])
            image = jnp.concatenate([low, zero], axis=0) + jnp.concatenate([zero, high], axis=0)
            correction = correction + inv * (rc - image)
        ends = [corners(correction[own - 1]), corners(correction[own])]
        for b in range(N):
            mid = {key: mix(((INTERP[b, j], ends[j][key]) for j in range(2))) for key in ends[0]}
            values = []
            for a in range(N - 1):
                pair = [mix(((INTERP[a, i], mid[i, k]) for i in range(2))) for k in range(2)]
                values.append([
                    sol[node(a, b, c)] + mix(((INTERP[c, k], pair[k]) for k in range(2)))
                    for c in range(N - 1)
                ])
            put_plane(b, values, sol)

    def face_copy(slot, side, at):
        return pltpu.make_async_remote_copy(
            src_ref=face.at[side], dst_ref=got.at[slot, 1 - side],
            send_sem=f_send.at[side], recv_sem=f_recv.at[slot, 1 - side],
            device_id=place(at), device_id_type=MESH)

    def face_wait(slot, side, at):
        pltpu.make_async_remote_copy(
            src_ref=face.at[side], dst_ref=got.at[slot, side],
            send_sem=f_send.at[side], recv_sem=f_recv.at[slot, side],
            device_id=place(at), device_id_type=MESH).wait()

    def both(fn):
        @pl.when(row >= 1)
        def _():
            fn(0, row - 1)

        @pl.when(row + 1 < rows)
        def _():
            fn(1, row + 1)

    def step(s, _):
        slot = lax.rem(s, 2)

        @pl.when((lax.rem(s, NPRE + NPOST) == NPRE) & (s < STEPS - 1))
        def _():
            coarse(s // (NPRE + NPOST))

        for side in range(2):
            summed = gather_plane(plane_local(side * (N - 1)))
            for a in range(N - 1):
                for c in range(N - 1):
                    face[side, a * 4 + c] = summed[a][c]
        both(lambda side, at: face_copy(slot, side, at).start())
        for b in range(1, N - 1):
            summed = gather_plane(plane_local(b))
            for a in range(N - 1):
                for c in range(N - 1):
                    total[(b * 4 + a) * 4 + c] = summed[a][c]
        scale = jnp.where(s < STEPS - 1, F32(1.0), F32(0.0))
        for b in range(1, N - 1):
            update_plane(b, scale)
        both(lambda side, at: face_wait(slot, side, at))
        for side in range(2):
            for i in range(16):
                total[side * (N - 1) * 16 + i] = face[side, i] + got[slot, side, i]
            update_plane(side * (N - 1), scale)
        return 0

    lax.fori_loop(0, STEPS, step, 0)

    for b in range(N):
        put_plane(b, [[total[(b * 4 + a) * 4 + c] for c in range(N - 1)] for a in range(N - 1)], load)

    def out(i, _):
        sol_out[i] = sol[i][0:layers]
        res_out[i] = load[i][0:layers]
        return 0

    lax.fori_loop(0, N * N * N, out, 0)


def per_device(sizes, load, kappa, wet):
    layers, _, width = kappa.shape
    nodes = N * N * N
    tile = (2 * layers, width)
    sizes = sizes + (layers, width)
    out = jax.ShapeDtypeStruct((nodes, layers, width), F32)
    vmem = pl.BlockSpec(memory_space=pltpu.VMEM)
    span = 2 * REACH + 1
    dma = pltpu.SemaphoreType.DMA
    solution, residual = pl.pallas_call(
        functools.partial(kernel, sizes),
        out_shape=(out, out),
        in_specs=[vmem] * 3,
        out_specs=(vmem, vmem),
        scratch_shapes=[
            pltpu.VMEM((nodes, layers, width), F32),
            pltpu.VMEM((layers, width), F32),
            pltpu.VMEM((layers, width), F32),
            pltpu.VMEM((nodes,) + tile, F32),
            pltpu.VMEM((span,) + tile, F32),
            pltpu.VMEM((nodes,) + tile, F32),
            pltpu.VMEM((N * 16,) + tile, F32),
            pltpu.VMEM((12,) + tile, F32),
            pltpu.VMEM((2 * REACH,) + tile, F32),
            pltpu.VMEM((2, 16) + tile, F32),
            pltpu.VMEM((2, 2, 16) + tile, F32),
            pltpu.VMEM((CYCLES, span, 2) + tile, F32),
            dma((2,)), dma((2,)), dma((span,)), dma((span,)),
            dma((2,)), dma((2, 2)), dma((span,)), dma((CYCLES, span)),
        ],
        compiler_params=pltpu.CompilerParams(collective_id=0, has_side_effects=True),
    )(load.reshape(nodes, layers, width), kappa.reshape(layers, width), wet.reshape(layers, width))
    return solution.reshape(load.shape), residual.reshape(load.shape)


def solution(mesh):
    sizes = tuple(mesh.shape[name] for name in ("ex", "ey", "lin"))
    field = P(None, None, None, None, ("ey", "lin"), "ex")
    cell = P(None, ("ey", "lin"), "ex")
    return jax.shard_map(
        functools.partial(per_device, sizes), mesh=mesh, in_specs=(field, cell, cell),
        out_specs=(field, field), check_vma=False,
    )
```

time: 455 us -> 68.2 us (0.15); the launches traced: 447 us -> 68.1 us
  waiting for transfers between devices: 191 us -> 0 us
  starting transfers between devices: 164 us -> 0 us
  Pallas kernels: 0 us -> 65 us
  matrix products: 62 us -> 0 us
  other arithmetic: 12.6 us -> 0 us
  local copies, waits for them, and re-layouts: 12.5 us -> 2.41 us
    ppermute x76 -> x0, waiting for transfers between devices: 191 us -> none  [the longest x38 162 us: padded_2(): lax.ppermute(head, axis, [((i + 1) % count, i) for i in range(ends)])]
    ppermute x76 -> x0, starting transfers between devices: 164 us -> none  [the longest x38 99.9 us: padded_2(): lax.ppermute(tail, axis, [(i, (i + 1) % count) for i in range(ends)])]
    pallas_call x0 -> x1, Pallas kernels: none -> 65 us  [per_device(): pl.pallas_call(functools.partial(kernel, sizes), out_shape=(out, out), in...]
    dot_general x140 -> x0, matrix products: 62 us -> none  [the longest x52 23.3 us: along(): jnp.einsum('pa,a...->p...', matrix, field, precision=lax.Precision.HIGHEST)]
    add x91 -> x0, other arithmetic: 5.09 us -> none  [the longest x38 1.88 us: pair_sum(): lax.slice_in_dim(upper, 0, length - 1, axis=elem_axis)]
  transfers between devices with their start and end apart: 76 -> 0, of which waited for: 66 -> 0; matrix products, arithmetic and copies ran while one was open for 3% -> 0% of each run, Pallas kernels for 0% -> 0%
where the time goes in v1:
time: 68.2 us; the launch traced here: 68.1 us
  Pallas kernels  65 us (95%)
  local copies, waits for them, and re-layouts  2.41 us (4%)
    pallas_call x1, Pallas kernels, per_device(): pl.pallas_call(functools.partial(kernel, sizes), out_shape=(out, out), in...  65 us
    unnamed x4, local copies, waits for them, and re-layouts  2.41 us

profile of v1, /device:TPU:25, one launch (start us, length us, event | category | flops | bytes accessed | tf_op | source)
XLA Modules:
  0.0 68.1 jit_solution(2420899438938856102)
XLA Ops:
  0.6 65.0 %shard_map.50 = (f32[125,4,128]{2,1,0:T(4,128)}, f32[125,4,128]{2,1,0:T(4,128)}) custom-call(f32[125,4,128]{2,1,0:T(4,128)} %bitcast.9, f32[4,128]{1,0:T(4,128)} %bitcast.12, s32[4,128]{1,0:T(4,128)} %bitcast.13), custom_call_target="tpu_custom_call" | custom-call | tf_op jit(solution)/shard_map/pallas_call | solution.py:401
  65.6 0.0 copy-start
  65.7 1.7 %copy.9 = f32[5,5,5,4,1,128]{5,4,3,2,1,0:T(1,128)} copy(f32[5,5,5,4,1,128]{5,4,3,2,1,0:T(1,128)} %bitcast.11) | data formatting | bytes 512000
  67.4 0.0 copy-done
  67.4 0.7 %copy.10 = f32[5,5,5,4,1,128]{5,4,3,2,1,0:T(1,128)} copy(f32[5,5,5,4,1,128]{5,4,3,2,1,0:T(1,128)S(1)} %bitcast.10) | data formatting | bytes 512000
Async XLA Ops:
  65.6 1.7 %copy-start = (f32[125,4,128]{2,1,0:T(4,128)S(1)}, f32[125,4,128]{2,1,0:T(4,128)}, u32[]{:S(2)}) copy-start(f32[125,4,128]{2,1,0:T(4,128)} %get-tuple-element.5) | copy-start | bytes 768004

commit v2 on v1

--- a/solution.py
+++ b/solution.py
@@ -16,7 +16,7 @@
 NC = 4
 FINE_RELAX = 0.25
 COARSE_RELAX = 0.4
-REACH = NC
+REACH = NC + 1
 STEPS = CYCLES * (NPRE + NPOST) + 1
 HALO = 32
 MESH = pl.DeviceIdType.MESH
@@ -180,21 +180,21 @@
         return 0
 
     lax.fori_loop(0, N * N * N, join, 0)
-    partners(k_wait)
-
     def inverted(x):
         return jnp.where(x > 0.0, 1.0 / jnp.where(x > 0.0, x, 1.0), 0.0)
 
-    here = coeffs[own]
-    for kind, x in enumerate((here, here + coeffs[own - 1], here + coeffs[own + 1])):
-        xc = x + before(x)
-        for slot, y in enumerate((x, xc, below(x, x), below(xc, xc))):
-            inverse[kind * 4 + slot] = inverted(y)
-    pairs = coeffs[0:2 * REACH] + coeffs[1:2 * REACH + 1]
-    pairs = pairs + before(pairs)
-    pairs = below(pairs, pairs)
-    corner = 3.0 * COARSE_STIFF[0, 0] * COARSE_MASS[0, 0] ** 2
-    cinv[...] = float(COARSE_RELAX / corner) * inverted(pairs)
+    def invert():
+        partners(k_wait)
+        here = coeffs[own]
+        for kind, x in enumerate((here, here + coeffs[own - 1], here + coeffs[own + 1])):
+            xc = x + before(x)
+            for slot, y in enumerate((x, xc, below(x, x), below(xc, xc))):
+                inverse[kind * 4 + slot] = inverted(y)
+        pairs = coeffs[0:2 * REACH] + coeffs[1:2 * REACH + 1]
+        pairs = pairs + before(pairs)
+        pairs = below(pairs, pairs)
+        corner = 3.0 * COARSE_STIFF[0, 0] * COARSE_MASS[0, 0] ** 2
+        cinv[...] = float(COARSE_RELAX / corner) * inverted(pairs)
 
     def plane_local(b):
         v = [[sol[node(a, b, c)] for c in range(N)] for a in range(N)]
@@ -258,26 +258,29 @@
             send_sem=c_send.at[mine], recv_sem=c_recv.at[cycle, mine],
             device_id=place(at), device_id_type=MESH).wait()
 
-    def coarse(cycle):
+    def gather(q, j):
+        h = [q[i, j, 0] + before(q[i, j, 1]) for i in range(2)]
+        return below(h[0], h[1])
+
+    def coarse_send(cycle):
         q = {}
         for b in range(N):
-            f = plane_local(b)
-            g = [[mix((INTERP[c, k], f[a][c]) for c in range(N)) for k in range(2)] for a in range(N)]
+            side = {0: 0, N - 1: 1}.get(b)
+            f = [[total[(b * 4 + a) * 4 + c] if side is None else face[side, a * 4 + c]
+                  for c in range(N - 1)] for a in range(N - 1)]
+            g = [[mix((INTERP[c, k], f[a][c]) for c in range(N - 1)) for k in range(2)] for a in range(N - 1)]
             for i in range(2):
                 for k in range(2):
-                    h = mix((INTERP[a, i], g[a][k]) for a in range(N))
+                    h = mix((INTERP[a, i], g[a][k]) for a in range(N - 1))
                     for j in range(2):
                         if INTERP[b, j] != 0:
                             term = scaled(INTERP[b, j], h)
                             q[i, j, k] = q[i, j, k] + term if (i, j, k) in q else term
-
-        def gather(q, j):
-            h = [q[i, j, 0] + before(q[i, j, 1]) for i in range(2)]
-            return below(h[0], h[1])
-
         for j in range(2):
             cgot[cycle, own, j] = gather(q, j)
         partners(lambda *p: c_copy(cycle, *p).start())
+
+    def correct(cycle):
         partners(lambda *p: c_wait(cycle, *p))
         lines = 2 * REACH
         rc = cgot[cycle, 0:lines, 1] + cgot[cycle, 1:lines + 1, 0]
@@ -315,17 +318,55 @@
             zero = jnp.zeros_like(low[0:1])
             image = jnp.concatenate([low, zero], axis=0) + jnp.concatenate([zero, high], axis=0)
             correction = correction + inv * (rc - image)
-        ends = [corners(correction[own - 1]), corners(correction[own])]
+        ends = [corners(correction[own - 2 + m]) for m in range(4)]
+
+        def interpolated(k, b):
+            return {key: mix(((INTERP[b, j], ends[k + j][key]) for j in range(2))) for key in ends[0]}
+
+        def operated(k, b):
+            coeff = coeffs[own - 1 + k]
+            half = {key: (0.5 * coeff) * value for key, value in interpolated(k, b).items()}
+            f = [[None] * N for _ in range(N)]
+
+            def put(a, c, value):
+                f[a][c] = value if f[a][c] is None else f[a][c] + value
+
+            rise_c = [half[i, 1] - half[i, 0] for i in range(2)]
+            rise_a = [half[1, i] - half[0, i] for i in range(2)]
+            for n in range(N):
+                value = float(WEIGHTS[n] * WEIGHTS[b]) * mix(((INTERP[n, i], rise_c[i]) for i in range(2)))
+                put(n, 0, value)
+                put(n, N - 1, -value)
+                value = float(WEIGHTS[n] * WEIGHTS[b]) * mix(((INTERP[n, i], rise_a[i]) for i in range(2)))
+                put(0, n, value)
+                put(N - 1, n, -value)
+            if b in (0, N - 1):
+                sign = 0.5 if b == 0 else -0.5
+                rise_b = {key: (sign * coeff) * (ends[k + 1][key] - ends[k][key]) for key in ends[0]}
+                for a in range(N):
+                    pair = [mix(((INTERP[a, i], rise_b[i, x]) for i in range(2))) for x in range(2)]
+                    for c in range(N):
+                        put(a, c, float(WEIGHTS[a] * WEIGHTS[c]) * mix(((INTERP[c, x], pair[x]) for x in range(2))))
+            return f
+
         for b in range(N):
-            mid = {key: mix(((INTERP[b, j], ends[j][key]) for j in range(2))) for key in ends[0]}
-            values = []
+            sums = [gather_plane(operated(1, b))]
+            if b == 0:
+                sums.append(gather_plane(operated(0, N - 1)))
+            if b == N - 1:
+                sums.append(gather_plane(operated(2, 0)))
+            mid = interpolated(1, b)
             for a in range(N - 1):
                 pair = [mix(((INTERP[a, i], mid[i, k]) for i in range(2))) for k in range(2)]
-                values.append([
-                    sol[node(a, b, c)] + mix(((INTERP[c, k], pair[k]) for k in range(2)))
-                    for c in range(N - 1)
-                ])
-            put_plane(b, values, sol)
+                for c in range(N - 1):
+                    at = node(a, b, c)
+                    sol[at] = sol[at] + mix(((INTERP[c, k], pair[k]) for k in range(2)))
+                    if sums[0][a][c] is not None:
+                        at = (b * 4 + a) * 4 + c
+                        value = total[at]
+                        for one in sums:
+                            value = value + one[a][c]
+                        total[at] = value
 
     def face_copy(slot, side, at):
         return pltpu.make_async_remote_copy(
@@ -351,9 +392,8 @@
     def step(s, _):
         slot = lax.rem(s, 2)
 
-        @pl.when((lax.rem(s, NPRE + NPOST) == NPRE) & (s < STEPS - 1))
-        def _():
-            coarse(s // (NPRE + NPOST))
+        cycle = s // (NPRE + NPOST)
+        coarse = (lax.rem(s, NPRE + NPOST) == NPRE) & (s < STEPS - 1)
 
         for side in range(2):
             summed = gather_plane(plane_local(side * (N - 1)))
@@ -367,12 +407,32 @@
                 for c in range(N - 1):
                     total[(b * 4 + a) * 4 + c] = summed[a][c]
         scale = jnp.where(s < STEPS - 1, F32(1.0), F32(0.0))
-        for b in range(1, N - 1):
-            update_plane(b, scale)
+
+        @pl.when(s == 0)
+        def _():
+            invert()
+
+        @pl.when(coarse)
+        def _():
+            coarse_send(cycle)
+
+        @pl.when(jnp.logical_not(coarse))
+        def _():
+            for b in range(1, N - 1):
+                update_plane(b, scale)
+
         both(lambda side, at: face_wait(slot, side, at))
         for side in range(2):
             for i in range(16):
                 total[side * (N - 1) * 16 + i] = face[side, i] + got[slot, side, i]
+
+        @pl.when(coarse)
+        def _():
+            correct(cycle)
+            for b in range(1, N - 1):
+                update_plane(b, scale)
+
+        for side in range(2):
             update_plane(side * (N - 1), scale)
         return 0
 

time: 68.2 us -> 61.4 us (0.900)
  Pallas kernels: 65 us -> 57.7 us
    pallas_call x1, Pallas kernels: 65 us -> 57.7 us  [per_device(): pl.pallas_call(functools.partial(kernel, sizes), out_shape=(out, out), in...]
where the time goes in v2:
time: 61.4 us; the launch traced here: 60.7 us
  Pallas kernels  57.7 us (94%)
  local copies, waits for them, and re-layouts  2.41 us (4%)
  between operations  0.65 us (1%)
    pallas_call x1, Pallas kernels, per_device(): pl.pallas_call(functools.partial(kernel, sizes), out_shape=(out, out), in...  57.7 us
    unnamed x4, local copies, waits for them, and re-layouts  2.41 us

profile of v2, /device:TPU:25, one launch (start us, length us, event | category | flops | bytes accessed | tf_op | source)
XLA Modules:
  0.0 60.7 jit_solution(2362849052773588253)
XLA Ops:
  0.6 57.7 %shard_map.50 = (f32[125,4,128]{2,1,0:T(4,128)}, f32[125,4,128]{2,1,0:T(4,128)}) custom-call(f32[125,4,128]{2,1,0:T(4,128)} %bitcast.9, f32[4,128]{1,0:T(4,128)} %bitcast.12, s32[4,128]{1,0:T(4,128)} %bitcast.13), custom_call_target="tpu_custom_call" | custom-call | tf_op jit(solution)/shard_map/pallas_call | solution.py:461
  58.3 0.0 copy-start
  58.3 1.7 %copy.9 = f32[5,5,5,4,1,128]{5,4,3,2,1,0:T(1,128)} copy(f32[5,5,5,4,1,128]{5,4,3,2,1,0:T(1,128)} %bitcast.11) | data formatting | bytes 512000
  60.0 0.0 copy-done
  60.0 0.7 %copy.10 = f32[5,5,5,4,1,128]{5,4,3,2,1,0:T(1,128)} copy(f32[5,5,5,4,1,128]{5,4,3,2,1,0:T(1,128)S(1)} %bitcast.10) | data formatting | bytes 512000
Async XLA Ops:
  58.3 1.7 %copy-start = (f32[125,4,128]{2,1,0:T(4,128)S(1)}, f32[125,4,128]{2,1,0:T(4,128)}, u32[]{:S(2)}) copy-start(f32[125,4,128]{2,1,0:T(4,128)} %get-tuple-element.5) | copy-start | bytes 768004

commit v3 on v2

--- a/solution.py
+++ b/solution.py
@@ -87,7 +87,7 @@
 
 def kernel(
     sizes, load_ref, kappa_ref, wet_ref, sol_out, res_out,
-    other_load, other_coeff, own_coeff, load, coeffs, sol, total, inverse, cinv, face, got, cgot,
+    other_load, other_coeff, own_coeff, load, coeffs, sol, total, inverse, cinv, face, packed, got, cgot,
     ex_send, ex_recv, k_send, k_recv, f_send, f_recv, c_send, c_recv,
 ):
     ex_count, ey_count, lin_count, layers, width = sizes
@@ -368,15 +368,48 @@
                             value = value + one[a][c]
                         total[at] = value
 
+    fold = width // HALO
+    block = lax.rem(lane + jnp.where(ex == 0, 0, HALO - 1), width) // HALO
+    lower = sub < layers
+
+    def swap(x):
+        return pltpu.roll(x, layers, 0)
+
+    def pack(side, x):
+        for p in range(8):
+            packed[side, p] = jnp.where(lower, x[2 * p], swap(x[2 * p + 1]))
+        for p in range(8 // fold):
+            halves = []
+            for h in range(2):
+                group = x[(2 * p + h) * fold:(2 * p + h + 1) * fold]
+                mixed = group[0]
+                for j in range(1, fold):
+                    mixed = jnp.where(block == j, pltpu.roll(group[j], HALO * j, 1), mixed)
+                halves.append(mixed)
+            packed[side, 8 + p] = jnp.where(lower, swap(halves[0]), halves[1])
+
+    def unpack(slot, side):
+        x = []
+        for p in range(8 // fold):
+            tile = got[slot, side, 8 + p]
+            for half in (swap(tile), tile):
+                for j in range(fold):
+                    other = half if j == 0 else pltpu.roll(half, width - HALO * j, 1)
+                    n = len(x)
+                    mine = got[slot, side, n // 2]
+                    mine = mine if n % 2 == 0 else swap(mine)
+                    x.append(jnp.where(lower, mine, jnp.where(block == 0, other, 0.0)))
+        return x
+
     def face_copy(slot, side, at):
         return pltpu.make_async_remote_copy(
-            src_ref=face.at[side], dst_ref=got.at[slot, 1 - side],
+            src_ref=packed.at[side], dst_ref=got.at[slot, 1 - side],
             send_sem=f_send.at[side], recv_sem=f_recv.at[slot, 1 - side],
             device_id=place(at), device_id_type=MESH)
 
     def face_wait(slot, side, at):
         pltpu.make_async_remote_copy(
-            src_ref=face.at[side], dst_ref=got.at[slot, side],
+            src_ref=packed.at[side], dst_ref=got.at[slot, side],
             send_sem=f_send.at[side], recv_sem=f_recv.at[slot, side],
             device_id=place(at), device_id_type=MESH).wait()
 
@@ -400,6 +433,7 @@
             for a in range(N - 1):
                 for c in range(N - 1):
                     face[side, a * 4 + c] = summed[a][c]
+            pack(side, [value for values in summed for value in values])
         both(lambda side, at: face_copy(slot, side, at).start())
         for b in range(1, N - 1):
             summed = gather_plane(plane_local(b))
@@ -423,8 +457,9 @@
 
         both(lambda side, at: face_wait(slot, side, at))
         for side in range(2):
+            theirs = unpack(slot, side)
             for i in range(16):
-                total[side * (N - 1) * 16 + i] = face[side, i] + got[slot, side, i]
+                total[side * (N - 1) * 16 + i] = face[side, i] + theirs[i]
 
         @pl.when(coarse)
         def _():
@@ -457,6 +492,7 @@
     out = jax.ShapeDtypeStruct((nodes, layers, width), F32)
     vmem = pl.BlockSpec(memory_space=pltpu.VMEM)
     span = 2 * REACH + 1
+    messages = 8 + 8 * HALO // width
     dma = pltpu.SemaphoreType.DMA
     solution, residual = pl.pallas_call(
         functools.partial(kernel, sizes),
@@ -474,7 +510,8 @@
             pltpu.VMEM((12,) + tile, F32),
             pltpu.VMEM((2 * REACH,) + tile, F32),
             pltpu.VMEM((2, 16) + tile, F32),
-            pltpu.VMEM((2, 2, 16) + tile, F32),
+            pltpu.VMEM((2, messages) + tile, F32),
+            pltpu.VMEM((2, 2, messages) + tile, F32),
             pltpu.VMEM((CYCLES, span, 2) + tile, F32),
             dma((2,)), dma((2,)), dma((span,)), dma((span,)),
             dma((2,)), dma((2, 2)), dma((span,)), dma((CYCLES, span)),

time: 61.4 us -> 59.5 us (0.969)
  Pallas kernels: 57.7 us -> 56.2 us
    pallas_call x1, Pallas kernels: 57.7 us -> 56.2 us  [per_device(): pl.pallas_call(functools.partial(kernel, sizes), out_shape=(out, out), in...]
where the time goes in v3:
time: 59.5 us; the launch traced here: 59.3 us
  Pallas kernels  56.2 us (94%)
  local copies, waits for them, and re-layouts  2.41 us (4%)
  between operations  0.65 us (1%)
    pallas_call x1, Pallas kernels, per_device(): pl.pallas_call(functools.partial(kernel, sizes), out_shape=(out, out), in...  56.2 us
    unnamed x4, local copies, waits for them, and re-layouts  2.41 us

profile of v3, /device:TPU:25, one launch (start us, length us, event | category | flops | bytes accessed | tf_op | source)
XLA Modules:
  0.0 59.3 jit_solution(493180894540204317)
XLA Ops:
  0.6 56.2 %shard_map.50 = (f32[125,4,128]{2,1,0:T(4,128)}, f32[125,4,128]{2,1,0:T(4,128)}) custom-call(f32[125,4,128]{2,1,0:T(4,128)} %bitcast.9, f32[4,128]{1,0:T(4,128)} %bitcast.12, s32[4,128]{1,0:T(4,128)} %bitcast.13), custom_call_target="tpu_custom_call" | custom-call | tf_op jit(solution)/shard_map/pallas_call | solution.py:497
  56.9 0.0 copy-start
  56.9 1.7 %copy.9 = f32[5,5,5,4,1,128]{5,4,3,2,1,0:T(1,128)} copy(f32[5,5,5,4,1,128]{5,4,3,2,1,0:T(1,128)} %bitcast.11) | data formatting | bytes 512000
  58.6 0.0 copy-done
  58.6 0.7 %copy.10 = f32[5,5,5,4,1,128]{5,4,3,2,1,0:T(1,128)} copy(f32[5,5,5,4,1,128]{5,4,3,2,1,0:T(1,128)S(1)} %bitcast.10) | data formatting | bytes 512000
Async XLA Ops:
  56.9 1.7 %copy-start = (f32[125,4,128]{2,1,0:T(4,128)S(1)}, f32[125,4,128]{2,1,0:T(4,128)}, u32[]{:S(2)}) copy-start(f32[125,4,128]{2,1,0:T(4,128)} %get-tuple-element.5) | copy-start | bytes 768004

commit v4 on v3

--- a/solution.py
+++ b/solution.py
@@ -176,10 +176,12 @@
     load_copy.wait()
 
     def join(i, _):
-        load[i] = jnp.where(real, jnp.concatenate([load_ref[i], other_load[i]], axis=0), 0.0)
+        for k in range(N * N):
+            at = i * N * N + k
+            load[at] = jnp.where(real, jnp.concatenate([load_ref[at], other_load[at]], axis=0), 0.0)
         return 0
 
-    lax.fori_loop(0, N * N * N, join, 0)
+    lax.fori_loop(0, N, join, 0)
     def inverted(x):
         return jnp.where(x > 0.0, 1.0 / jnp.where(x > 0.0, x, 1.0), 0.0)
 
@@ -477,11 +479,13 @@
         put_plane(b, [[total[(b * 4 + a) * 4 + c] for c in range(N - 1)] for a in range(N - 1)], load)
 
     def out(i, _):
-        sol_out[i] = sol[i][0:layers]
-        res_out[i] = load[i][0:layers]
+        for k in range(N * N):
+            at = i * N * N + k
+            sol_out[at] = sol[at][0:layers]
+            res_out[at] = load[at][0:layers]
         return 0
 
-    lax.fori_loop(0, N * N * N, out, 0)
+    lax.fori_loop(0, N, out, 0)
 
 
 def per_device(sizes, load, kappa, wet):

time: 59.5 us -> 58 us (0.975)
  Pallas kernels: 56.2 us -> 54.7 us
    pallas_call x1, Pallas kernels: 56.2 us -> 54.7 us  [per_device(): pl.pallas_call(functools.partial(kernel, sizes), out_shape=(out, out), in...]
where the time goes in v4:
time: 58 us; the launch traced here: 57.7 us
  Pallas kernels  54.7 us (94%)
  local copies, waits for them, and re-layouts  2.41 us (4%)
  between operations  0.65 us (1%)
    pallas_call x1, Pallas kernels, per_device(): pl.pallas_call(functools.partial(kernel, sizes), out_shape=(out, out), in...  54.7 us
    unnamed x4, local copies, waits for them, and re-layouts  2.41 us

profile of v4, /device:TPU:25, one launch (start us, length us, event | category | flops | bytes accessed | tf_op | source)
XLA Modules:
  0.0 57.7 jit_solution(12819081522678891903)
XLA Ops:
  0.6 54.7 %shard_map.50 = (f32[125,4,128]{2,1,0:T(4,128)}, f32[125,4,128]{2,1,0:T(4,128)}) custom-call(f32[125,4,128]{2,1,0:T(4,128)} %bitcast.9, f32[4,128]{1,0:T(4,128)} %bitcast.12, s32[4,128]{1,0:T(4,128)} %bitcast.13), custom_call_target="tpu_custom_call" | custom-call | tf_op jit(solution)/shard_map/pallas_call | solution.py:501
  55.3 0.0 copy-start
  55.3 1.7 %copy.9 = f32[5,5,5,4,1,128]{5,4,3,2,1,0:T(1,128)} copy(f32[5,5,5,4,1,128]{5,4,3,2,1,0:T(1,128)} %bitcast.11) | data formatting | bytes 512000
  57.0 0.0 copy-done
  57.0 0.7 %copy.10 = f32[5,5,5,4,1,128]{5,4,3,2,1,0:T(1,128)} copy(f32[5,5,5,4,1,128]{5,4,3,2,1,0:T(1,128)S(1)} %bitcast.10) | data formatting | bytes 512000
Async XLA Ops:
  55.3 1.7 %copy-start = (f32[125,4,128]{2,1,0:T(4,128)S(1)}, f32[125,4,128]{2,1,0:T(4,128)}, u32[]{:S(2)}) copy-start(f32[125,4,128]{2,1,0:T(4,128)} %get-tuple-element.5) | copy-start | bytes 768004
